TPU v7x, 512 devices: a whole 4x4x16 slice. The times are simulated.
512 devices in a mesh: dp: 64 (over z, x_lo, core), lon: 8 (over y, x_hi).
Axes of the slice: x: 4 (x_hi: 2, x_lo: 2; x = x_hi * 2 + x_lo), y: 4, z: 16, core: 2. Of those that a mesh axis runs over, the one named last changes fastest.
Arguments:
- features: bfloat16 [64, 72, 48, 1152], P('dp', 'lon'), may hold values from -6 to 6
- depth_w: bfloat16 [2, 3, 3, 1152], replicated, may hold values from -2 to 2
- point_w: bfloat16 [2, 1152, 256], replicated, may hold values from -0.1875 to 0.1875
- point_bias: float32 [2, 256], replicated, may hold values from -3 to 3
- cotangent: bfloat16 [64, 72, 48, 512], P('dp', 'lon'), may hold values from -6 to 6
Outputs:
- feature_grad: bfloat16 [64, 72, 48, 1152], P('dp', 'lon')
- depth_grad: bfloat16 [2, 3, 3, 1152], replicated
- point_grad: bfloat16 [2, 1152, 256], replicated
- bias_grad: float32 [2, 256], replicated
All inputs are finite; a program needn't handle non-finite values.
Results may differ from a plain program's by a relative error of at most 0.0075.
Values may be sent and summed in bfloat16 or wider, within the bound.
No kernel may reach another device: no remote copies, remote signals or barrier semaphores. Data moves between devices by JAX's collectives and lax.ppermute only.
A program may use at most 128 MiB of HBM per device.

v0:
```python
import jax
import jax.numpy as jnp
from jax import lax
from jax.sharding import PartitionSpec as P

RATE_A = 24
RATE_B = 36


def from_behind(block, axis, distance):
    devices = range(lax.axis_size(axis))
    route = [((i - distance) % len(devices), i) for i in devices]
    return lax.ppermute(block, axis, route)


def lat_shift(grid_field, offset, axis_pos):
    height = grid_field.shape[axis_pos]
    if offset == 0:
        return grid_field
    widths = [(0, 0)] * grid_field.ndim
    if offset > 0:
        kept_rows = lax.slice_in_dim(grid_field, offset, height, axis=axis_pos)
        widths[axis_pos] = (0, offset)
    else:
        kept_rows = lax.slice_in_dim(grid_field, 0, height + offset, axis=axis_pos)
        widths[axis_pos] = (-offset, 0)
    return jnp.pad(kept_rows, widths)


def gate_slope(pre_act):
    sigmoid_val = jax.nn.sigmoid(pre_act)
    return sigmoid_val * (1.0 + pre_act * (1.0 - sigmoid_val))


def column_plan(dilation, direction, columns, group_size):
    run_list = []
    for column in range(columns):
        target = column + direction * dilation
        offset = target // columns
        local_col = target % columns
        if run_list and run_list[-1][0] == offset:
            run_list[-1][2] = local_col + 1
        else:
            run_list.append([offset, local_col, local_col + 1])
    return [(-entry[0] % group_size, entry[1], entry[2]) for entry in run_list]


def join_pieces(piece_list):
    if len(piece_list) == 1:
        return piece_list[0]
    return jnp.concatenate(piece_list, axis=1)


def fetch_each(grid_field, offset_pairs, group_size, send_fn):
    result = {}
    for offset_pair in offset_pairs:
        piece_list = []
        for shift_by, first_col, finish in column_plan(
            offset_pair[0], offset_pair[1], grid_field.shape[1], group_size
        ):
            column_piece = grid_field[:, first_col:finish]
            column_piece = send_fn(column_piece, shift_by)
            piece_list.append(column_piece)
        result[offset_pair] = join_pieces(piece_list)
    return result


def send_features(column_piece, shift_by):
    return from_behind(column_piece, "lon", shift_by)


def send_grads(column_piece, shift_by):
    return from_behind(column_piece, "lon", shift_by)


def per_device(features, depth_w, point_w, point_bias, cotangent):
    group_size = lax.axis_size("lon")
    channels = features.shape[3]
    outputs = point_w.shape[2]
    dilations = (RATE_A, RATE_B)
    offset_pairs = [(dilation, direction) for dilation in dilations for direction in (-1, 1)]
    moved_in = fetch_each(features, offset_pairs, group_size, send_features)
    depth_outs = []
    for branch, dilation in enumerate(dilations):
        depth_acc = jnp.zeros(features.shape, jnp.float32)
        for lon_step in (-1, 0, 1):
            source = features if lon_step == 0 else moved_in[dilation, lon_step]
            for lat_step in (-1, 0, 1):
                tapped = lat_shift(source, lat_step * dilation, 2).astype(jnp.float32)
                depth_acc = (
                    depth_acc
                    + depth_w[branch, lat_step + 1, lon_step + 1].astype(jnp.float32) * tapped
                )
        depth_outs.append(depth_acc.astype(jnp.bfloat16))
    point_terms = []
    bias_terms = []
    dgrad_list = []
    for branch, dilation in enumerate(dilations):
        flat_depth = depth_outs[branch].reshape(-1, channels)
        point_act = (
            jnp.dot(flat_depth, point_w[branch], preferred_element_type=jnp.float32)
            + point_bias[branch]
        )
        upstream_part = (
            cotangent[..., branch * outputs : (branch + 1) * outputs]
            .reshape(-1, outputs)
            .astype(jnp.float32)
        )
        pgrad = (upstream_part * gate_slope(point_act)).astype(jnp.bfloat16)
        bias_terms.append(jnp.sum(pgrad.astype(jnp.float32), axis=0))
        point_terms.append(
            lax.dot_general(
                flat_depth, pgrad, (((0,), (0,)), ((), ())), preferred_element_type=jnp.float32
            )
        )
        dgrad = lax.dot_general(
            pgrad, point_w[branch], (((1,), (1,)), ((), ())), preferred_element_type=jnp.float32
        )
        dgrad_list.append(dgrad.astype(jnp.bfloat16).reshape(features.shape))
    point_local = jnp.stack(point_terms)
    bias_local = jnp.stack(bias_terms)
    grad_field = jnp.zeros(features.shape, jnp.float32)
    depth_terms = []
    for branch, dilation in enumerate(dilations):
        branch_pairs = [(dilation, -1), (dilation, 1)]
        moved_back = fetch_each(dgrad_list[branch], branch_pairs, group_size, send_grads)
        dgrad_wide = dgrad_list[branch].astype(jnp.float32)
        tap_rows = []
        for lat_step in (-1, 0, 1):
            tap_cols = []
            for lon_step in (-1, 0, 1):
                source = features if lon_step == 0 else moved_in[dilation, lon_step]
                tapped = lat_shift(source, lat_step * dilation, 2).astype(jnp.float32)
                tap_cols.append(jnp.sum(tapped * dgrad_wide, axis=(0, 1, 2)))
                behind = dgrad_list[branch] if lon_step == 0 else moved_back[dilation, -lon_step]
                behind = lat_shift(behind, -lat_step * dilation, 2).astype(jnp.float32)
                grad_field = (
                    grad_field
                    + depth_w[branch, lat_step + 1, lon_step + 1].astype(jnp.float32) * behind
                )
            tap_rows.append(jnp.stack(tap_cols))
        depth_terms.append(jnp.stack(tap_rows))
    depth_local = jnp.stack(depth_terms)
    feature_grad = grad_field.astype(jnp.bfloat16)
    point_sum, depth_sum, bias_sum = lax.psum((point_local, depth_local, bias_local), ("dp", "lon"))
    images = lax.axis_size("dp") * features.shape[0]
    depth_grad = (depth_sum / images).astype(jnp.bfloat16)
    point_grad = (point_sum / images).astype(jnp.bfloat16)
    bias_grad = bias_sum / images
    return (feature_grad, depth_grad, point_grad, bias_grad)


def solution(mesh):
    placed = (P("dp", "lon", None, None), P(), P(), P(), P("dp", "lon", None, None))
    return jax.shard_map(
        per_device,
        mesh=mesh,
        in_specs=placed,
        out_specs=(P("dp", "lon", None, None), P(), P(), P()),
        check_vma=False,
    )
```

profile of v0, /device:TPU:1, one launch (start us, length us, event | category | flops | bytes accessed | tf_op | source)
XLA Modules:
  0.0 733.2 jit_solution(12406998658973591604)
XLA Ops:
  7.2 5.8 collective-permute-start.8
  13.0 1.4 fusion.71
  14.4 4.8 collective-permute-start
  19.3 2.1 collective-permute-start.1
  21.3 5.4 collective-permute-start.3
  26.8 3.0 collective-permute-start.2
  30.3 42.3 %collective-permute-done.2 = bf16[1,3,48,1152]{3,2,1,0:T(8,128)(2,1)S(1)} collective-permute-done((bf16[1,3,48,1152]{3,2,1,0:T(8,128)(2,1)S(1)}, bf16[1,3,48,1152]{3,2,1,0:T(8,128)(2,1)S(1)}, u32[]{:S(2)}, u32[]{:S(2)}) %collective-permute-start.2) | collective-permute-done | bytes 331808 | tf_op jit(solution)/shard_map/ppermute | solution.py:13
  73.1 1.5 fusion.8
  75.2 0.7 fusion.26
  75.9 1.2 fusion.67
  77.0 0.8 fusion.68
  77.9 3.3 collective-permute-start.4
  81.2 0.9 fusion.63
  83.3 4.4 collective-permute-start.5
  87.7 3.3 collective-permute-start.6
  91.0 2.0 collective-permute-start.7
  93.0 1.5 convolution_bitcast_fusion.1
  94.5 0.8 constant_dynamic-update-slice_fusion.5
  95.4 1.4 fusion.15
  97.3 1.6 convolution_bitcast_fusion
  99.3 4.3 collective-permute-start.9
  103.6 2.3 fusion.41
  106.1 139.6 %psum.23 = f32[2,256]{1,0:T(2,128)S(1)} all-reduce(f32[2,256]{1,0:T(2,128)S(1)} %pad_maximum_fusion.2), channel_id=1, replica_groups=mesh['dp'=64,'lon'=8] {'dp','lon'}, use_global_device_ids=true, to_apply=%region_19.20 | all-reduce | flops 512 | bytes 4096 | tf_op jit(solution)/shard_map/psum | solution.py:145
  245.7 3.2 pad_maximum_fusion
  249.1 0.7 pad_maximum_fusion.1
  250.5 1.1 constant_dynamic-update-slice_fusion.7
  251.6 1.2 constant_dynamic-update-slice_fusion.4
  252.8 1.0 constant_dynamic-update-slice_fusion.6
  254.1 1.2 fusion.65
  255.5 5.0 fusion.25
  260.5 462.3 %all-reduce.23.cloned.1.call-done = (f32[2,3,3,1152]{3,2,1,0:T(4,128)}, f32[2,1152,256]{2,1,0:T(8,128)}) async-done(((f32[2,3,3,1152]{3,2,1,0:T(4,128)}, f32[2,1152,256]{2,1,0:T(8,128)}), (f32[2,3,3,1152]{3,2,1,0:T(4,128)}, f32[2,1152,256]{2,1,0:T(8,128)})) %all-reduce.23.cloned.1.call-update) | async-done | bytes 2442256 | tf_op jit(solution)/shard_map/psum | solution.py:145
  722.7 2.9 multiply_convert_fusion
  (115 shorter events, 5.6 us)
Async XLA Ops:
  7.2 12.0 %copy-start = (bf16[1,9,48,1152]{3,2,1,0:T(8,128)(2,1)S(1)}, bf16[1,9,48,1152]{3,2,1,0:T(8,128)(2,1)}, u32[]{:S(2)}) copy-start(bf16[1,9,48,1152]{3,2,1,0:T(8,128)(2,1)} %param.5) | copy-start | bytes 2985988
  7.2 715.6 %all-reduce.23.cloned.1.call-start = ((), (), s32[]{:S(2)}) async-start(), calls=%async_computation | async-start | bytes 4939776 | tf_op jit(solution)/shard_map/psum | solution.py:145
  7.2 88.0 %collective-permute-start.8 = (bf16[1,9,48,1152]{3,2,1,0:T(8,128)(2,1)}, bf16[1,9,48,1152]{3,2,1,0:T(8,128)(2,1)S(1)}, u32[]{:S(2)}, u32[]{:S(2)}) collective-permute-start(bf16[1,9,48,1152]{3,2,1,0:T(8,128)(2,1)} %param.5), channel_id=1, source_target_pairs={{4,0},{5,1},{6,2},{7,3},{0,4},{1,5},{2,6},{3,7},{12,8},{13,9},{14,... | collective-permute-start | bytes 2985992 | tf_op jit(solution)/shard_map/ppermute | solution.py:13
  14.4 58.2 %collective-permute-start = (bf16[1,6,48,1152]{3,2,1,0:T(8,128)(2,1)S(1)}, bf16[1,6,48,1152]{3,2,1,0:T(8,128)(2,1)S(1)}, u32[]{:S(2)}, u32[]{:S(2)}) collective-permute-start(bf16[1,6,48,1152]{3,2,1,0:T(8,128)(2,1)S(1)} %get-tuple-element.61), channel_id=1, source_target_pairs={{5,0},{6,1},{7,2},{0,3},{1,4},{2,5},{3,6},{4,7},{13,8},{14,9},{15,... | collective-permute-start | bytes 1990664 | tf_op jit(solution)/shard_map/ppermute | solution.py:13
  19.3 10.7 %copy-start.29 = (f32[2,256]{1,0:T(2,128)S(1)}, f32[2,256]{1,0:T(2,128)}, u32[]{:S(2)}) copy-start(f32[2,256]{1,0:T(2,128)} %param.8) | copy-start | bytes 6148
  19.3 10.7 %copy-start.5 = (bf16[2,3,3,1152]{3,0,2,1:T(2,128)(2,1)S(1)}, bf16[2,3,3,1152]{3,0,2,1:T(2,128)(2,1)}, u32[]{:S(2)}) copy-start(bf16[2,3,3,1152]{3,0,2,1:T(2,128)(2,1)} %param.6) | copy-start | bytes 124420
  19.3 10.9 %copy-start.3 = (bf16[1,9,48,512]{3,2,1,0:T(8,128)(2,1)S(1)}, bf16[1,9,48,512]{3,2,1,0:T(8,128)(2,1)}, u32[]{:S(2)}) copy-start(bf16[1,9,48,512]{3,2,1,0:T(8,128)(2,1)} %param.9) | copy-start | bytes 1327108
  19.3 53.4 %collective-permute-start.1 = (bf16[1,3,48,1152]{3,2,1,0:T(8,128)(2,1)S(1)}, bf16[1,3,48,1152]{3,2,1,0:T(8,128)(2,1)S(1)}, u32[]{:S(2)}, u32[]{:S(2)}) collective-permute-start(bf16[1,3,48,1152]{3,2,1,0:T(8,128)(2,1)S(1)} %get-tuple-element.59), channel_id=1, source_target_pairs={{6,0},{7,1},{0,2},{1,3},{2,4},{3,5},{4,6},{5,7},{14,8},{15,9},{8,1... | collective-permute-start | bytes 995336 | tf_op jit(solution)/shard_map/ppermute | solution.py:13
  21.3 51.5 %collective-permute-start.3 = (bf16[1,6,48,1152]{3,2,1,0:T(8,128)(2,1)S(1)}, bf16[1,6,48,1152]{3,2,1,0:T(8,128)(2,1)S(1)}, u32[]{:S(2)}, u32[]{:S(2)}) collective-permute-start(bf16[1,6,48,1152]{3,2,1,0:T(8,128)(2,1)S(1)} %get-tuple-element.62), channel_id=1, source_target_pairs={{3,0},{4,1},{5,2},{6,3},{7,4},{0,5},{1,6},{2,7},{11,8},{12,9},{13,... | collective-permute-start | bytes 1990664 | tf_op jit(solution)/shard_map/ppermute | solution.py:13
  26.8 45.8 %collective-permute-start.2 = (bf16[1,3,48,1152]{3,2,1,0:T(8,128)(2,1)S(1)}, bf16[1,3,48,1152]{3,2,1,0:T(8,128)(2,1)S(1)}, u32[]{:S(2)}, u32[]{:S(2)}) collective-permute-start(bf16[1,3,48,1152]{3,2,1,0:T(8,128)(2,1)S(1)} %get-tuple-element.60), channel_id=1, source_target_pairs={{2,0},{3,1},{4,2},{5,3},{6,4},{7,5},{0,6},{1,7},{10,8},{11,9},{12,... | collective-permute-start | bytes 995336 | tf_op jit(solution)/shard_map/ppermute | solution.py:13
  30.2 42.8 %copy-start.9 = (f32[1152]{0:T(1024)}, f32[1152]{0:T(1024)S(1)}, u32[]{:S(2)}) copy-start(f32[1152]{0:T(1024)S(1)} %get-tuple-element.23) | copy-start | bytes 13828
  30.2 42.8 %copy-start.11 = (f32[1152]{0:T(1024)}, f32[1152]{0:T(1024)S(1)}, u32[]{:S(2)}) copy-start(f32[1152]{0:T(1024)S(1)} %get-tuple-element.31) | copy-start | bytes 13828
  30.2 42.8 %copy-start.13 = (f32[1152]{0:T(1024)}, f32[1152]{0:T(1024)S(1)}, u32[]{:S(2)}) copy-start(f32[1152]{0:T(1024)S(1)} %get-tuple-element.32) | copy-start | bytes 13828
  30.2 42.8 %copy-start.15 = (f32[1152]{0:T(1024)}, f32[1152]{0:T(1024)S(1)}, u32[]{:S(2)}) copy-start(f32[1152]{0:T(1024)S(1)} %get-tuple-element.33) | copy-start | bytes 13828
  30.2 42.8 %copy-start.17 = (f32[1152]{0:T(1024)}, f32[1152]{0:T(1024)S(1)}, u32[]{:S(2)}) copy-start(f32[1152]{0:T(1024)S(1)} %get-tuple-element.34) | copy-start | bytes 13828
  30.3 42.8 %copy-start.19 = (f32[1152]{0:T(1024)}, f32[1152]{0:T(1024)S(1)}, u32[]{:S(2)}) copy-start(f32[1152]{0:T(1024)S(1)} %get-tuple-element.35) | copy-start | bytes 13828
  30.3 42.8 %copy-start.21 = (f32[1152]{0:T(1024)}, f32[1152]{0:T(1024)S(1)}, u32[]{:S(2)}) copy-start(f32[1152]{0:T(1024)S(1)} %get-tuple-element.36) | copy-start | bytes 13828
  30.3 42.8 %copy-start.23 = (f32[1152]{0:T(1024)}, f32[1152]{0:T(1024)S(1)}, u32[]{:S(2)}) copy-start(f32[1152]{0:T(1024)S(1)} %get-tuple-element.37) | copy-start | bytes 13828
  30.3 42.8 %copy-start.25 = (f32[1152]{0:T(1024)}, f32[1152]{0:T(1024)S(1)}, u32[]{:S(2)}) copy-start(f32[1152]{0:T(1024)S(1)} %get-tuple-element.38) | copy-start | bytes 13828
  30.3 65.1 %copy-start.7 = (f32[1152]{0:T(1024)}, f32[1152]{0:T(1024)S(1)}, u32[]{:S(2)}) copy-start(f32[1152]{0:T(1024)S(1)} %get-tuple-element.40) | copy-start | bytes 13828
  73.1 1.5 copy-start.4
  77.9 16.6 %collective-permute-start.4 = (bf16[1,3,48,1152]{3,2,1,0:T(8,128)(2,1)S(1)}, bf16[1,3,48,1152]{3,2,1,0:T(8,128)(2,1)S(1)}, u32[]{:S(2)}, u32[]{:S(2)}) collective-permute-start(bf16[1,3,48,1152]{3,2,1,0:T(8,128)(2,1)S(1)} %get-tuple-element.55), channel_id=1, source_target_pairs={{2,0},{3,1},{4,2},{5,3},{6,4},{7,5},{0,6},{1,7},{10,8},{11,9},{12,... | collective-permute-start | bytes 995336 | tf_op jit(solution)/shard_map/ppermute | solution.py:13
  83.3 168.3 %collective-permute-start.5 = (bf16[1,6,48,1152]{3,2,1,0:T(8,128)(2,1)}, bf16[1,6,48,1152]{3,2,1,0:T(8,128)(2,1)}, u32[]{:S(2)}, u32[]{:S(2)}) collective-permute-start(bf16[1,6,48,1152]{3,2,1,0:T(8,128)(2,1)} %get-tuple-element.53), channel_id=1, source_target_pairs={{3,0},{4,1},{5,2},{6,3},{7,4},{0,5},{1,6},{2,7},{11,8},{12,9},{13,... | collective-permute-start | bytes 1990664 | tf_op jit(solution)/shard_map/ppermute | solution.py:13
  87.7 162.7 %collective-permute-start.6 = (bf16[1,6,48,1152]{3,2,1,0:T(8,128)(2,1)}, bf16[1,6,48,1152]{3,2,1,0:T(8,128)(2,1)}, u32[]{:S(2)}, u32[]{:S(2)}) collective-permute-start(bf16[1,6,48,1152]{3,2,1,0:T(8,128)(2,1)} %get-tuple-element.54), channel_id=1, source_target_pairs={{5,0},{6,1},{7,2},{0,3},{1,4},{2,5},{3,6},{4,7},{13,8},{14,9},{15,... | collective-permute-start | bytes 1990664 | tf_op jit(solution)/shard_map/ppermute | solution.py:13
  91.0 161.8 %collective-permute-start.7 = (bf16[1,3,48,1152]{3,2,1,0:T(8,128)(2,1)}, bf16[1,3,48,1152]{3,2,1,0:T(8,128)(2,1)}, u32[]{:S(2)}, u32[]{:S(2)}) collective-permute-start(bf16[1,3,48,1152]{3,2,1,0:T(8,128)(2,1)} %get-tuple-element.56), channel_id=1, source_target_pairs={{6,0},{7,1},{0,2},{1,3},{2,4},{3,5},{4,6},{5,7},{14,8},{15,9},{8,1... | collective-permute-start | bytes 995336 | tf_op jit(solution)/shard_map/ppermute | solution.py:13
  99.3 154.8 %collective-permute-start.9 = (bf16[1,9,48,1152]{3,2,1,0:T(8,128)(2,1)S(1)}, bf16[1,9,48,1152]{3,2,1,0:T(8,128)(2,1)}, u32[]{:S(2)}, u32[]{:S(2)}) collective-permute-start(bf16[1,9,48,1152]{3,2,1,0:T(8,128)(2,1)S(1)} %bitcast.69), channel_id=1, source_target_pairs={{4,0},{5,1},{6,2},{7,3},{0,4},{1,5},{2,6},{3,7},{12,8},{13,9},{14,... | collective-permute-start | bytes 2985992 | tf_op jit(solution)/shard_map/ppermute | solution.py:13
  245.7 3.3 copy-start.27
  245.7 3.3 copy-start.28
  249.8 1.9 copy-start.1
  253.9 1.4 copy-start.2
  253.9 1.4 copy-start.8
  722.7 2.9 copy-start.6
  (9 other events, 12.9 us)
Sparse Core Ops, SparseCore 0:
  249.9 472.7 all-reduce.22
where the time goes:
time: 734 us; the launch traced here: 733 us
  waiting for transfers between devices  505 us (69%)
  blocking collectives  140 us (19%)
  starting transfers between devices  38.2 us (5%)
  other arithmetic  17.9 us (2%)
  between operations  14.9 us (2%)
  local copies, waits for them, and re-layouts  12.6 us (2%)
    psum x1, waiting for transfers between devices, per_device(): lax.psum((point_local, depth_local, bias_local), ('dp', 'lon'))  462 us
    psum x1, blocking collectives, per_device(): lax.psum((point_local, depth_local, bias_local), ('dp', 'lon'))  140 us
    ppermute x10, waiting for transfers between devices, from_behind(): return lax.ppermute(block, axis, route)  42.3 us
    ppermute x10, starting transfers between devices, from_behind(): return lax.ppermute(block, axis, route)  38.2 us
  transfers between devices with their start and end apart: 11, of which 2 were waited for; matrix products, arithmetic and copies ran while one was open for 4% of the time, Pallas kernels for 0%

commit v1 on v0

--- a/solution.py
+++ b/solution.py
@@ -2,6 +2,7 @@
 import jax.numpy as jnp
 from jax import lax
 from jax.sharding import PartitionSpec as P
+from jax.lax import psum
 
 RATE_A = 24
 RATE_B = 36
@@ -142,7 +143,13 @@
         depth_terms.append(jnp.stack(tap_rows))
     depth_local = jnp.stack(depth_terms)
     feature_grad = grad_field.astype(jnp.bfloat16)
-    point_sum, depth_sum, bias_sum = lax.psum((point_local, depth_local, bias_local), ("dp", "lon"))
+
+    def fix_the_object(s0):
+        for d in ("dp", "lon"):
+            s0 = psum(s0, axis_name=d)
+        return s0
+
+    point_sum, depth_sum, bias_sum = fix_the_object((point_local, depth_local, bias_local))
     images = lax.axis_size("dp") * features.shape[0]
     depth_grad = (depth_sum / images).astype(jnp.bfloat16)
     point_grad = (point_sum / images).astype(jnp.bfloat16)

time: 734 us -> 701 us (0.955)
  waiting for transfers between devices: 505 us -> 484 us
  blocking collectives: 140 us -> 129 us
    psum x1 -> x2, waiting for transfers between devices: 462 us -> 423 us  [fix_the_object(): s0 = psum(s0, axis_name=d)]
    ppermute x10, waiting for transfers between devices: 42.3 us -> 61.1 us  [from_behind(): return lax.ppermute(block, axis, route)]
    psum x1 -> x2, blocking collectives: 140 us -> 129 us  [fix_the_object(): s0 = psum(s0, axis_name=d)]
  transfers between devices with their start and end apart: 11 -> 12, of which waited for: 2 -> 4; matrix products, arithmetic and copies ran while one was open for 4% -> 4% of each run, Pallas kernels for 0% -> 0%
where the time goes in v1:
time: 701 us; the launch traced here: 700 us
  waiting for transfers between devices  484 us (69%)
  blocking collectives  129 us (18%)
  starting transfers between devices  36.7 us (5%)
  other arithmetic  16.9 us (2%)
  between operations  15 us (2%)
  local copies, waits for them, and re-layouts  13.9 us (2%)
    psum x2, waiting for transfers between devices, fix_the_object(): s0 = psum(s0, axis_name=d)  423 us
    psum x2, blocking collectives, fix_the_object(): s0 = psum(s0, axis_name=d)  129 us
    ppermute x10, waiting for transfers between devices, from_behind(): return lax.ppermute(block, axis, route)  61.1 us
    ppermute x10, starting transfers between devices, from_behind(): return lax.ppermute(block, axis, route)  36.7 us
  transfers between devices with their start and end apart: 12, of which 4 were waited for; matrix products, arithmetic and copies ran while one was open for 4% of the time, Pallas kernels for 0%

profile of v1, /device:TPU:1, one launch (start us, length us, event | category | flops | bytes accessed | tf_op | source)
XLA Modules:
  0.0 700.2 jit_solution(16211761667689777323)
XLA Ops:
  7.2 5.8 collective-permute-start.8
  13.0 1.4 fusion.71
  14.4 4.8 collective-permute-start
  19.3 2.1 collective-permute-start.1
  21.3 5.4 collective-permute-start.3
  26.8 3.0 collective-permute-start.2
  30.3 42.3 %collective-permute-done.2 = bf16[1,3,48,1152]{3,2,1,0:T(8,128)(2,1)S(1)} collective-permute-done((bf16[1,3,48,1152]{3,2,1,0:T(8,128)(2,1)S(1)}, bf16[1,3,48,1152]{3,2,1,0:T(8,128)(2,1)S(1)}, u32[]{:S(2)}, u32[]{:S(2)}) %collective-permute-start.2) | collective-permute-done | bytes 331808 | tf_op jit(solution)/shard_map/ppermute | solution.py:14
  73.1 1.5 fusion.8
  74.6 1.2 convert_reduce_fusion.1
  76.5 1.2 fusion.67
  77.6 5.8 collective-permute-start.5
  84.4 2.1 collective-permute-start.4
  86.6 3.0 collective-permute-start.6
  89.6 2.0 collective-permute-start.7
  92.3 1.4 fusion.15
  93.7 1.1 convert_reduce_fusion
  95.8 2.3 fusion.41
  98.3 1.5 pad_maximum_fusion
  101.6 18.8 %collective-permute-done.4 = bf16[1,3,48,1152]{3,2,1,0:T(8,128)(2,1)} collective-permute-done((bf16[1,3,48,1152]{3,2,1,0:T(8,128)(2,1)}, bf16[1,3,48,1152]{3,2,1,0:T(8,128)(2,1)}, u32[]{:S(2)}, u32[]{:S(2)}) %collective-permute-start.4) | collective-permute-done | bytes 331808 | tf_op jit(solution)/shard_map/ppermute | solution.py:14
  120.4 1.0 constant_dynamic-update-slice_fusion.5
  121.4 2.7 collective-permute-start.9
  124.8 112.2 %psum.46 = f32[2,256]{1,0:T(2,128)} all-reduce(f32[2,256]{1,0:T(2,128)S(1)} %pad_maximum_fusion.2), channel_id=1, replica_groups=mesh['dp'=64,'lon'=8] {'dp'}, use_global_device_ids=true, to_apply=%region_21.22 | all-reduce | flops 512 | bytes 4096 | tf_op jit(solution)/shard_map/psum | solution.py:149
  236.9 16.7 %psum.47 = f32[2,256]{1,0:T(2,128)S(1)} all-reduce(f32[2,256]{1,0:T(2,128)} %psum.46), channel_id=1, replica_groups=mesh['dp'=64,'lon'=8] {'lon'}, use_global_device_ids=true, to_apply=%region_22.23 | all-reduce | flops 512 | bytes 4096 | tf_op jit(solution)/shard_map/psum | solution.py:149
  255.2 1.2 constant_dynamic-update-slice_fusion.4
  256.3 1.1 fusion.62
  257.6 1.1 constant_dynamic-update-slice_fusion.7
  258.8 290.5 %all-reduce.25.cloned.1.call-done = (f32[2,3,3,1152]{3,2,1,0:T(4,128)}, f32[2,1152,256]{2,1,0:T(8,128)}) async-done(((f32[2,3,3,1152]{3,2,1,0:T(4,128)}, f32[2,1152,256]{2,1,0:T(8,128)}), (f32[2,3,3,1152]{3,2,1,0:T(4,128)}, f32[2,1152,256]{2,1,0:T(8,128)})) %all-reduce.25.cloned.1.call-update) | async-done | bytes 2442256 | tf_op jit(solution)/shard_map/psum | solution.py:149
  549.5 1.2 constant_dynamic-update-slice_fusion.6
  550.7 1.2 fusion.65
  552.1 5.0 fusion.25
  557.1 132.7 %all-reduce.27.cloned.1.call-done = (f32[2,3,3,1152]{3,2,1,0:T(4,128)}, f32[2,1152,256]{2,1,0:T(8,128)}) async-done(((f32[2,3,3,1152]{3,2,1,0:T(4,128)}, f32[2,1152,256]{2,1,0:T(8,128)}), (f32[2,3,3,1152]{3,2,1,0:T(4,128)}, f32[2,1152,256]{2,1,0:T(8,128)})) %all-reduce.27.cloned.1.call-update) | async-done | bytes 2442256 | tf_op jit(solution)/shard_map/psum | solution.py:149
  689.8 2.9 multiply_convert_fusion
  (125 shorter events, 9.3 us)
Async XLA Ops:
  7.2 12.0 %copy-start = (bf16[1,9,48,1152]{3,2,1,0:T(8,128)(2,1)S(1)}, bf16[1,9,48,1152]{3,2,1,0:T(8,128)(2,1)}, u32[]{:S(2)}) copy-start(bf16[1,9,48,1152]{3,2,1,0:T(8,128)(2,1)} %param.5) | copy-start | bytes 2985988
  7.2 542.1 %all-reduce.25.cloned.1.call-start = ((), (), s32[]{:S(2)}) async-start(), calls=%async_computation | async-start | bytes 4939776 | tf_op jit(solution)/shard_map/psum | solution.py:149
  7.2 84.9 %collective-permute-start.8 = (bf16[1,9,48,1152]{3,2,1,0:T(8,128)(2,1)}, bf16[1,9,48,1152]{3,2,1,0:T(8,128)(2,1)S(1)}, u32[]{:S(2)}, u32[]{:S(2)}) collective-permute-start(bf16[1,9,48,1152]{3,2,1,0:T(8,128)(2,1)} %param.5), channel_id=1, source_target_pairs={{4,0},{5,1},{6,2},{7,3},{0,4},{1,5},{2,6},{3,7},{12,8},{13,9},{14,... | collective-permute-start | bytes 2985992 | tf_op jit(solution)/shard_map/ppermute | solution.py:14
  14.4 58.2 %collective-permute-start = (bf16[1,6,48,1152]{3,2,1,0:T(8,128)(2,1)S(1)}, bf16[1,6,48,1152]{3,2,1,0:T(8,128)(2,1)S(1)}, u32[]{:S(2)}, u32[]{:S(2)}) collective-permute-start(bf16[1,6,48,1152]{3,2,1,0:T(8,128)(2,1)S(1)} %get-tuple-element.63), channel_id=1, source_target_pairs={{5,0},{6,1},{7,2},{0,3},{1,4},{2,5},{3,6},{4,7},{13,8},{14,9},{15,... | collective-permute-start | bytes 1990664 | tf_op jit(solution)/shard_map/ppermute | solution.py:14
  19.3 10.7 %copy-start.32 = (f32[2,256]{1,0:T(2,128)S(1)}, f32[2,256]{1,0:T(2,128)}, u32[]{:S(2)}) copy-start(f32[2,256]{1,0:T(2,128)} %param.8) | copy-start | bytes 6148
  19.3 10.7 %copy-start.10 = (bf16[2,3,3,1152]{3,0,2,1:T(2,128)(2,1)S(1)}, bf16[2,3,3,1152]{3,0,2,1:T(2,128)(2,1)}, u32[]{:S(2)}) copy-start(bf16[2,3,3,1152]{3,0,2,1:T(2,128)(2,1)} %param.6) | copy-start | bytes 124420
  19.3 10.9 %copy-start.8 = (bf16[1,9,48,512]{3,2,1,0:T(8,128)(2,1)S(1)}, bf16[1,9,48,512]{3,2,1,0:T(8,128)(2,1)}, u32[]{:S(2)}) copy-start(bf16[1,9,48,512]{3,2,1,0:T(8,128)(2,1)} %param.9) | copy-start | bytes 1327108
  19.3 53.4 %collective-permute-start.1 = (bf16[1,3,48,1152]{3,2,1,0:T(8,128)(2,1)S(1)}, bf16[1,3,48,1152]{3,2,1,0:T(8,128)(2,1)S(1)}, u32[]{:S(2)}, u32[]{:S(2)}) collective-permute-start(bf16[1,3,48,1152]{3,2,1,0:T(8,128)(2,1)S(1)} %get-tuple-element.61), channel_id=1, source_target_pairs={{6,0},{7,1},{0,2},{1,3},{2,4},{3,5},{4,6},{5,7},{14,8},{15,9},{8,1... | collective-permute-start | bytes 995336 | tf_op jit(solution)/shard_map/ppermute | solution.py:14
  21.3 51.5 %collective-permute-start.3 = (bf16[1,6,48,1152]{3,2,1,0:T(8,128)(2,1)S(1)}, bf16[1,6,48,1152]{3,2,1,0:T(8,128)(2,1)S(1)}, u32[]{:S(2)}, u32[]{:S(2)}) collective-permute-start(bf16[1,6,48,1152]{3,2,1,0:T(8,128)(2,1)S(1)} %get-tuple-element.64), channel_id=1, source_target_pairs={{3,0},{4,1},{5,2},{6,3},{7,4},{0,5},{1,6},{2,7},{11,8},{12,9},{13,... | collective-permute-start | bytes 1990664 | tf_op jit(solution)/shard_map/ppermute | solution.py:14
  26.8 45.8 %collective-permute-start.2 = (bf16[1,3,48,1152]{3,2,1,0:T(8,128)(2,1)S(1)}, bf16[1,3,48,1152]{3,2,1,0:T(8,128)(2,1)S(1)}, u32[]{:S(2)}, u32[]{:S(2)}) collective-permute-start(bf16[1,3,48,1152]{3,2,1,0:T(8,128)(2,1)S(1)} %get-tuple-element.62), channel_id=1, source_target_pairs={{2,0},{3,1},{4,2},{5,3},{6,4},{7,5},{0,6},{1,7},{10,8},{11,9},{12,... | collective-permute-start | bytes 995336 | tf_op jit(solution)/shard_map/ppermute | solution.py:14
  30.2 42.8 %copy-start.14 = (f32[1152]{0:T(1024)}, f32[1152]{0:T(1024)S(1)}, u32[]{:S(2)}) copy-start(f32[1152]{0:T(1024)S(1)} %get-tuple-element.23) | copy-start | bytes 13828
  30.2 42.8 %copy-start.16 = (f32[1152]{0:T(1024)}, f32[1152]{0:T(1024)S(1)}, u32[]{:S(2)}) copy-start(f32[1152]{0:T(1024)S(1)} %get-tuple-element.31) | copy-start | bytes 13828
  30.2 42.8 %copy-start.18 = (f32[1152]{0:T(1024)}, f32[1152]{0:T(1024)S(1)}, u32[]{:S(2)}) copy-start(f32[1152]{0:T(1024)S(1)} %get-tuple-element.32) | copy-start | bytes 13828
  30.2 42.8 %copy-start.20 = (f32[1152]{0:T(1024)}, f32[1152]{0:T(1024)S(1)}, u32[]{:S(2)}) copy-start(f32[1152]{0:T(1024)S(1)} %get-tuple-element.33) | copy-start | bytes 13828
  30.2 42.8 %copy-start.22 = (f32[1152]{0:T(1024)}, f32[1152]{0:T(1024)S(1)}, u32[]{:S(2)}) copy-start(f32[1152]{0:T(1024)S(1)} %get-tuple-element.34) | copy-start | bytes 13828
  30.3 42.8 %copy-start.24 = (f32[1152]{0:T(1024)}, f32[1152]{0:T(1024)S(1)}, u32[]{:S(2)}) copy-start(f32[1152]{0:T(1024)S(1)} %get-tuple-element.35) | copy-start | bytes 13828
  30.3 42.8 %copy-start.26 = (f32[1152]{0:T(1024)}, f32[1152]{0:T(1024)S(1)}, u32[]{:S(2)}) copy-start(f32[1152]{0:T(1024)S(1)} %get-tuple-element.36) | copy-start | bytes 13828
  30.3 42.8 %copy-start.28 = (f32[1152]{0:T(1024)}, f32[1152]{0:T(1024)S(1)}, u32[]{:S(2)}) copy-start(f32[1152]{0:T(1024)S(1)} %get-tuple-element.37) | copy-start | bytes 13828
  30.3 42.8 %copy-start.30 = (f32[1152]{0:T(1024)}, f32[1152]{0:T(1024)S(1)}, u32[]{:S(2)}) copy-start(f32[1152]{0:T(1024)S(1)} %get-tuple-element.38) | copy-start | bytes 13828
  30.3 62.0 %copy-start.12 = (f32[1152]{0:T(1024)}, f32[1152]{0:T(1024)S(1)}, u32[]{:S(2)}) copy-start(f32[1152]{0:T(1024)S(1)} %get-tuple-element.40) | copy-start | bytes 13828
  77.6 177.5 %collective-permute-start.5 = (bf16[1,6,48,1152]{3,2,1,0:T(8,128)(2,1)}, bf16[1,6,48,1152]{3,2,1,0:T(8,128)(2,1)}, u32[]{:S(2)}, u32[]{:S(2)}) collective-permute-start(bf16[1,6,48,1152]{3,2,1,0:T(8,128)(2,1)} %get-tuple-element.55), channel_id=1, source_target_pairs={{3,0},{4,1},{5,2},{6,3},{7,4},{0,5},{1,6},{2,7},{11,8},{12,9},{13,... | collective-permute-start | bytes 1990664 | tf_op jit(solution)/shard_map/ppermute | solution.py:14
  84.4 36.0 %collective-permute-start.4 = (bf16[1,3,48,1152]{3,2,1,0:T(8,128)(2,1)}, bf16[1,3,48,1152]{3,2,1,0:T(8,128)(2,1)}, u32[]{:S(2)}, u32[]{:S(2)}) collective-permute-start(bf16[1,3,48,1152]{3,2,1,0:T(8,128)(2,1)} %get-tuple-element.57), channel_id=1, source_target_pairs={{2,0},{3,1},{4,2},{5,3},{6,4},{7,5},{0,6},{1,7},{10,8},{11,9},{12,... | collective-permute-start | bytes 995336 | tf_op jit(solution)/shard_map/ppermute | solution.py:14
  86.6 171.1 %collective-permute-start.6 = (bf16[1,6,48,1152]{3,2,1,0:T(8,128)(2,1)}, bf16[1,6,48,1152]{3,2,1,0:T(8,128)(2,1)}, u32[]{:S(2)}, u32[]{:S(2)}) collective-permute-start(bf16[1,6,48,1152]{3,2,1,0:T(8,128)(2,1)} %get-tuple-element.56), channel_id=1, source_target_pairs={{5,0},{6,1},{7,2},{0,3},{1,4},{2,5},{3,6},{4,7},{13,8},{14,9},{15,... | collective-permute-start | bytes 1990664 | tf_op jit(solution)/shard_map/ppermute | solution.py:14
  89.6 459.9 %collective-permute-start.7 = (bf16[1,3,48,1152]{3,2,1,0:T(8,128)(2,1)}, bf16[1,3,48,1152]{3,2,1,0:T(8,128)(2,1)}, u32[]{:S(2)}, u32[]{:S(2)}) collective-permute-start(bf16[1,3,48,1152]{3,2,1,0:T(8,128)(2,1)} %get-tuple-element.58), channel_id=1, source_target_pairs={{6,0},{7,1},{0,2},{1,3},{2,4},{3,5},{4,6},{5,7},{14,8},{15,9},{8,1... | collective-permute-start | bytes 995336 | tf_op jit(solution)/shard_map/ppermute | solution.py:14
  100.7 589.1 %all-reduce.27.cloned.1.call-start = ((), (), s32[]{:S(2)}) async-start(), calls=%async_computation.1 | async-start | bytes 4939776 | tf_op jit(solution)/shard_map/psum | solution.py:149
  121.4 429.3 %collective-permute-start.9 = (bf16[1,9,48,1152]{3,2,1,0:T(8,128)(2,1)S(1)}, bf16[1,9,48,1152]{3,2,1,0:T(8,128)(2,1)}, u32[]{:S(2)}, u32[]{:S(2)}) collective-permute-start(bf16[1,9,48,1152]{3,2,1,0:T(8,128)(2,1)S(1)} %bitcast.70), channel_id=1, source_target_pairs={{4,0},{5,1},{6,2},{7,3},{0,4},{1,5},{2,6},{3,7},{12,8},{13,9},{14,... | collective-permute-start | bytes 2985992 | tf_op jit(solution)/shard_map/ppermute | solution.py:14
  549.3 2.6 copy-start.2
  549.3 2.6 copy-start.3
  549.3 2.6 copy-start.4
  549.3 2.6 copy-start.5
  549.3 2.6 copy-start.6
  689.7 2.9 copy-start.11
  (13 other events, 31.3 us)
Sparse Core Ops, SparseCore 0:
  100.8 448.4 all-reduce.24
  552.6 137.0 all-reduce.26
